TPU v7x, 512 devices: a whole 4x8x8 slice. The times are simulated.
512 devices in a mesh: dp: 2 (over z_hi), ctx: 32 (over z_lo, y), tp: 8 (over x, core).
Axes of the slice: x: 4, y: 8, z: 8 (z_hi: 2, z_lo: 4; z = z_hi * 4 + z_lo), core: 2. Of those that a mesh axis runs over, the one named last changes fastest.
Arguments:
- left_stream: bfloat16 [2, 4096, 4096], P('dp', 'ctx', 'tp'), may hold values from -6 to 6
- outer_gate: bfloat16 [2, 4096, 4096], P('dp', 'ctx', 'tp'), may hold values from -6 to 6
- value_stream: bfloat16 [2, 4096, 4096], P('dp', 'ctx', 'tp'), may hold values from -6 to 6
- residual: bfloat16 [2, 4096, 4096], P('dp', 'ctx', 'tp'), may hold values from -36 to 36
- long_filter: float32 [256, 128], P('tp'), may hold values from -2 to 2
- skip_weight: float32 [4096], P('tp'), may hold values from -1 to 1
- norm_gain: float32 [4096], P('tp'), may hold values from 0.1 to 1.9
- normed_grad: bfloat16 [2, 4096, 4096], P('dp', 'ctx', 'tp'), may hold values from -6 to 6
- attn_queries: bfloat16 [2, 4096, 4096], P('dp', 'ctx', 'tp'), may hold values from -6 to 6
- attn_keys: bfloat16 [2, 4096, 4096], P('dp', 'ctx', 'tp'), may hold values from -6 to 6
- attn_values: bfloat16 [2, 4096, 4096], P('dp', 'ctx', 'tp'), may hold values from -6 to 6
- attended_grad: bfloat16 [2, 4096, 4096], P('dp', 'ctx', 'tp'), may hold values from -6 to 6
Outputs:
- normed: bfloat16 [2, 4096, 4096], P('dp', 'ctx', 'tp')
- grad_left: bfloat16 [2, 4096, 4096], P('dp', 'ctx', 'tp')
- grad_outer: bfloat16 [2, 4096, 4096], P('dp', 'ctx', 'tp')
- grad_value: bfloat16 [2, 4096, 4096], P('dp', 'ctx', 'tp')
- grad_residual: bfloat16 [2, 4096, 4096], P('dp', 'ctx', 'tp')
- grad_filter: float32 [256, 128], P('tp')
- grad_skip: float32 [4096], P('tp')
- grad_gain: float32 [4096], P('tp')
- attended: bfloat16 [2, 4096, 4096], P('dp', 'ctx', 'tp')
- grad_queries: bfloat16 [2, 4096, 4096], P('dp', 'ctx', 'tp')
- grad_keys: bfloat16 [2, 4096, 4096], P('dp', 'ctx', 'tp')
- grad_values: bfloat16 [2, 4096, 4096], P('dp', 'ctx', 'tp')
All inputs are finite; a program needn't handle non-finite values.
Results may differ from a plain program's by a relative error of at most 0.024.
Values may be sent and summed in bfloat16 or wider, within the bound.
A program may use at most 128 MiB of HBM per device.

v0:
```python
import jax
import jax.numpy as jnp
from jax import lax
from jax.sharding import PartitionSpec as P

HEAD_DIM = 128


def passed_along(value, axis, steps):
    count = lax.axis_size(axis)
    initial, last = (max(0, -steps), min(count, count - steps))
    return lax.ppermute(value, axis, [(source, source + steps) for source in range(initial, last)])


def toeplitz(taps_rows, rows):
    groups, length = taps_rows.shape
    width = rows + length - 1
    padded = jnp.pad(taps_rows, ((0, 0), (0, width + 1 - length)))
    tiled = jnp.tile(padded, (1, rows))[:, : rows * width]
    return tiled.reshape(groups, rows, width)


def diagonals(matrix, length):
    groups, rows, width = matrix.shape
    flat = jnp.pad(matrix.reshape(groups, rows * width), ((0, 0), (0, rows)))
    return flat.reshape(groups, rows, width + 1)[:, :, :length]


def scores_block(query_rows, key_block, scale):
    return (
        jnp.einsum("rhd,khd->hrk", query_rows, key_block, preferred_element_type=jnp.float32)
        * scale
    )


def key_block_at(key_all, value_all, number, block, positions):
    begin = number * block
    keys_here = lax.dynamic_slice_in_dim(key_all, begin, block, 0)
    values_here = lax.dynamic_slice_in_dim(value_all, begin, block, 0)
    key_pos = begin + jnp.arange(block, dtype=jnp.int32)
    allowed = key_pos[None, :] <= positions[:, None]
    return (keys_here, values_here, allowed)


def attend_rows(query_rows, first_pos, key_all, value_all, block, scale):
    count_rows = query_rows.shape[0]
    heads_here = query_rows.shape[1]
    positions = first_pos + jnp.arange(count_rows, dtype=jnp.int32)
    needed = (first_pos + count_rows - 1) // block + 1

    def first_pass(number, carry):
        running, total = carry
        keys_here, values_here, allowed = key_block_at(key_all, value_all, number, block, positions)
        scores = jnp.where(allowed[None], scores_block(query_rows, keys_here, scale), -jnp.inf)
        newest = jnp.maximum(running, jnp.max(scores, axis=2))
        total = total * jnp.exp(running - newest) + jnp.sum(
            jnp.exp(scores - newest[:, :, None]), axis=2
        )
        return (newest, total)

    start_carry = (
        jnp.full((heads_here, count_rows), -jnp.inf, jnp.float32),
        jnp.zeros((heads_here, count_rows), jnp.float32),
    )
    running, total = lax.fori_loop(0, needed, first_pass, start_carry)
    log_norm = running + jnp.log(total)

    def second_pass(number, output):
        keys_here, values_here, allowed = key_block_at(key_all, value_all, number, block, positions)
        scores = jnp.where(allowed[None], scores_block(query_rows, keys_here, scale), -jnp.inf)
        weights = jnp.exp(scores - log_norm[:, :, None]).astype(jnp.bfloat16)
        return output + jnp.einsum(
            "hrk,khd->rhd", weights, values_here, preferred_element_type=jnp.float32
        )

    output = lax.fori_loop(0, needed, second_pass, jnp.zeros(query_rows.shape, jnp.float32))
    return (output, log_norm)


def shards(
    left_stream,
    outer_gate,
    value_stream,
    residual,
    long_filter,
    skip_weight,
    norm_gain,
    normed_grad,
    attn_queries,
    attn_keys,
    attn_values,
    attended_grad,
):
    rows = left_stream.shape[1]
    channels = left_stream.shape[2]
    groups = long_filter.shape[0]
    taps = long_filter.shape[1]
    per_group = channels // groups
    width = channels * lax.axis_size("tp")
    heads_here = attn_queries.shape[2] // HEAD_DIM
    scale = HEAD_DIM ** (-0.5)
    key_all, value_all = (
        lax.all_gather(attn_keys[0], "ctx", axis=0, tiled=True),
        lax.all_gather(attn_values[0], "ctx", axis=0, tiled=True),
    )
    seq_len = key_all.shape[0]
    key_all = key_all.reshape(seq_len, heads_here, HEAD_DIM)
    value_all = value_all.reshape(seq_len, heads_here, HEAD_DIM)
    left_values = left_stream[0].astype(jnp.float32)
    value_values = value_stream[0].astype(jnp.float32)
    gate_values = outer_gate[0].astype(jnp.float32)
    product = (left_values * value_values).astype(jnp.bfloat16)
    earlier = passed_along(product[rows - (taps - 1) :], "ctx", 1)
    extended_narrow = jnp.concatenate([earlier, product], axis=0).reshape(
        rows + taps - 1, groups, per_group
    )
    extended = extended_narrow.astype(jnp.float32)
    forward_band = toeplitz(long_filter[:, ::-1], rows)
    product_wide = product.astype(jnp.float32)
    mixed = jnp.einsum(
        "gts,sgc->tgc",
        forward_band,
        extended,
        precision=lax.Precision.HIGHEST,
        preferred_element_type=jnp.float32,
    ).reshape(rows, channels)
    mixed = mixed + skip_weight[None, :] * product_wide
    stream = residual[0].astype(jnp.float32) + gate_values * mixed
    square_total = lax.psum(jnp.sum(stream * stream, axis=1), "tp")
    inv_rms = lax.rsqrt(square_total / width + 1e-06)
    scaled = stream * inv_rms[:, None]
    normed = (scaled * norm_gain[None, :]).astype(jnp.bfloat16)
    upstream = normed_grad[0].astype(jnp.float32)
    gain_grad = upstream * norm_gain[None, :]
    norm_dot = lax.psum(jnp.sum(gain_grad * scaled, axis=1), "tp")
    stream_grad = inv_rms[:, None] * (gain_grad - scaled * norm_dot[:, None] / width)
    grad_residual = stream_grad.astype(jnp.bfloat16)
    grad_outer = (stream_grad * mixed).astype(jnp.bfloat16)
    gated = (stream_grad * gate_values).astype(jnp.bfloat16)
    later = passed_along(gated[: taps - 1], "ctx", -1)
    ahead = (
        jnp.concatenate([gated, later], axis=0)
        .astype(jnp.float32)
        .reshape(rows + taps - 1, groups, per_group)
    )
    backward_band = toeplitz(long_filter, rows)
    gated_wide = gated.astype(jnp.float32)
    product_grad = jnp.einsum(
        "gts,sgc->tgc",
        backward_band,
        ahead,
        precision=lax.Precision.HIGHEST,
        preferred_element_type=jnp.float32,
    ).reshape(rows, channels)
    product_grad = product_grad + skip_weight[None, :] * gated_wide
    grad_left = (product_grad * value_values).astype(jnp.bfloat16)
    grad_value = (product_grad * left_values).astype(jnp.bfloat16)
    correlation = jnp.einsum(
        "tgc,sgc->gts",
        gated.reshape(rows, groups, per_group),
        extended_narrow,
        preferred_element_type=jnp.float32,
    )
    filter_part = jnp.sum(diagonals(correlation, taps), axis=1)[:, ::-1]
    skip_part = jnp.sum(gated_wide * product_wide, axis=0)
    gain_part = jnp.sum(upstream * scaled, axis=0)
    filter_sum, skip_sum, gain_sum = lax.psum((filter_part, skip_part, gain_part), ("dp", "ctx"))
    devices = lax.axis_size("ctx")
    index = lax.axis_index("ctx")
    per_block = min(devices, max(1, 512 // rows))
    block = rows * per_block
    own_first = index * rows
    query_rows = attn_queries[0].reshape(rows, heads_here, HEAD_DIM)
    attended_wide, log_norm = attend_rows(query_rows, own_first, key_all, value_all, block, scale)
    attended = attended_wide.astype(jnp.bfloat16)
    out_grad = attended_grad[0].reshape(rows, heads_here, HEAD_DIM)
    delta = jnp.sum(out_grad.astype(jnp.float32) * attended.astype(jnp.float32), axis=2).T
    positions = own_first + jnp.arange(rows, dtype=jnp.int32)
    needed = (own_first + rows - 1) // block + 1

    def query_grad_step(number, running_sum):
        keys_here, values_here, allowed = key_block_at(key_all, value_all, number, block, positions)
        scores = jnp.where(allowed[None], scores_block(query_rows, keys_here, scale), -jnp.inf)
        weights = jnp.exp(scores - log_norm[:, :, None]).astype(jnp.bfloat16)
        value_dots = jnp.einsum(
            "rhd,khd->hrk", out_grad, values_here, preferred_element_type=jnp.float32
        )
        score_grad = (weights.astype(jnp.float32) * (value_dots - delta[:, :, None])).astype(
            jnp.bfloat16
        )
        return running_sum + jnp.einsum(
            "hrk,khd->rhd", score_grad, keys_here, preferred_element_type=jnp.float32
        )

    query_grad = lax.fori_loop(
        0, needed, query_grad_step, jnp.zeros((rows, heads_here, HEAD_DIM), jnp.float32)
    )
    grad_queries = (query_grad * scale).astype(jnp.bfloat16)
    stat_norm, stat_delta = (
        lax.all_gather(log_norm.T, "ctx", axis=0, tiled=True),
        lax.all_gather(delta.T, "ctx", axis=0, tiled=True),
    )
    key_own = attn_keys[0].reshape(rows, heads_here, HEAD_DIM)
    value_own = attn_values[0].reshape(rows, heads_here, HEAD_DIM)
    empty = jnp.zeros((rows, heads_here, HEAD_DIM), jnp.float32)
    piece_query = lax.all_gather(attn_queries[0], "ctx", axis=0, tiled=True)
    piece_grad = lax.all_gather(attended_grad[0], "ctx", axis=0, tiled=True)
    count = piece_query.shape[0]
    stride_rows = 512

    def process(number, totals):
        offset = number * stride_rows
        query_part = lax.dynamic_slice_in_dim(piece_query, offset, stride_rows, 0).reshape(
            stride_rows, heads_here, HEAD_DIM
        )
        grad_part = lax.dynamic_slice_in_dim(piece_grad, offset, stride_rows, 0).reshape(
            stride_rows, heads_here, HEAD_DIM
        )
        norm_part = lax.dynamic_slice_in_dim(stat_norm, offset, stride_rows, 0).T
        delta_part = lax.dynamic_slice_in_dim(stat_delta, offset, stride_rows, 0).T
        query_pos = offset + jnp.arange(stride_rows, dtype=jnp.int32)

        def compute(current):
            key_sum, value_sum = current
            allowed = positions[None, :] <= query_pos[:, None]
            scores = jnp.where(allowed[None], scores_block(query_part, key_own, scale), -jnp.inf)
            weights = jnp.exp(scores - norm_part[:, :, None]).astype(jnp.bfloat16)
            value_dots = jnp.einsum(
                "rhd,khd->hrk", grad_part, value_own, preferred_element_type=jnp.float32
            )
            score_grad = (
                weights.astype(jnp.float32) * (value_dots - delta_part[:, :, None])
            ).astype(jnp.bfloat16)
            value_sum = value_sum + jnp.einsum(
                "hrk,rhd->khd", weights, grad_part, preferred_element_type=jnp.float32
            )
            key_sum = key_sum + jnp.einsum(
                "hrk,rhd->khd", score_grad, query_part, preferred_element_type=jnp.float32
            )
            return (key_sum, value_sum)

        def unchanged(current):
            return current

        reaches = offset + stride_rows - 1 >= own_first
        return lax.cond(reaches, compute, unchanged, totals)

    key_sum, value_sum = lax.fori_loop(0, count // stride_rows, process, (empty, empty))
    grad_keys = (key_sum * scale).astype(jnp.bfloat16)
    grad_values = value_sum.astype(jnp.bfloat16)
    flat = (rows, heads_here * HEAD_DIM)
    return (
        normed[None],
        grad_left[None],
        grad_outer[None],
        grad_value[None],
        grad_residual[None],
        filter_sum,
        skip_sum,
        gain_sum,
        attended.reshape(flat)[None],
        grad_queries.reshape(flat)[None],
        grad_keys.reshape(flat)[None],
        grad_values.reshape(flat)[None],
    )


def solution(mesh):
    in_specs = (
        P("dp", "ctx", "tp"),
        P("dp", "ctx", "tp"),
        P("dp", "ctx", "tp"),
        P("dp", "ctx", "tp"),
        P("tp", None),
        P("tp"),
        P("tp"),
        P("dp", "ctx", "tp"),
        P("dp", "ctx", "tp"),
        P("dp", "ctx", "tp"),
        P("dp", "ctx", "tp"),
        P("dp", "ctx", "tp"),
    )
    out_specs = (
        P("dp", "ctx", "tp"),
        P("dp", "ctx", "tp"),
        P("dp", "ctx", "tp"),
        P("dp", "ctx", "tp"),
        P("dp", "ctx", "tp"),
        P("tp", None),
        P("tp"),
        P("tp"),
        P("dp", "ctx", "tp"),
        P("dp", "ctx", "tp"),
        P("dp", "ctx", "tp"),
        P("dp", "ctx", "tp"),
    )
    return jax.shard_map(shards, mesh=mesh, in_specs=in_specs, out_specs=out_specs, check_vma=False)
```

profile of v0, /device:TPU:8, one launch (start us, length us, event | category | flops | bytes accessed | tf_op | source)
XLA Modules:
  0.0 652.6 jit_solution(11089281187697373970)
XLA Ops:
  7.2 1.7 copy.130
  9.0 1.7 copy.129
  10.7 1.7 copy.131
  12.4 1.0 fusion.64
  13.5 3.5 collective-permute-start
  17.0 1.7 copy.137
  18.8 0.8 rev.6
  19.9 2.4 copy.177
  22.4 2.2 slice.25
  24.6 9.6 %reshape.385 = f32[32,128,255]{2,1,0:T(8,128)} reshape(f32[32,32640]{1,0:T(8,128)} %slice.25) | data formatting | bytes 8355840 | tf_op jit(solution)/shard_map/reshape | solution.py:20
  35.1 2.4 copy.178
  37.5 2.2 slice.27
  39.8 9.5 %reshape.389 = f32[32,128,255]{2,1,0:T(8,128)} reshape(f32[32,32640]{1,0:T(8,128)} %slice.27) | data formatting | bytes 8355840 | tf_op jit(solution)/shard_map/reshape | solution.py:20
  50.0 4.2 fusion.93
  54.5 14.4 %psum.35 = f32[128]{0:T(128)S(1)} all-reduce(f32[128]{0:T(128)S(1)} %get-tuple-element.951), channel_id=1, replica_groups=mesh['dp'=2,'ctx'=32,'tp'=8] {'tp'}, use_global_device_ids=true, to_apply=%region_1.2 | all-reduce | flops 128 | bytes 1024 | tf_op jit(solution)/shard_map/psum | solution.py:129
  69.1 12.6 %psum.36 = f32[128]{0:T(128)S(1)} all-reduce(f32[128]{0:T(128)S(1)} %get-tuple-element.871), channel_id=1, replica_groups=mesh['dp'=2,'ctx'=32,'tp'=8] {'tp'}, use_global_device_ids=true, to_apply=%region_3.4 | all-reduce | flops 128 | bytes 1024 | tf_op jit(solution)/shard_map/psum | solution.py:135
  81.9 3.1 fusion.81
  85.0 5.2 reshape.391
  90.3 2.5 pad.13
  92.7 3.3 copy.179
  96.0 4.8 collective-permute-start.1
  101.0 0.8 fusion.90
  101.8 1.8 slice_reduce_fusion
  103.7 278.5 %all-reduce.3 = (f32[32,128]{1,0:T(8,128)}, f32[512]{0:T(512)}, f32[512]{0:T(512)}) all-reduce(f32[32,128]{1,0:T(8,128)S(1)} %rev.7, f32[512]{0:T(512)S(1)} %get-tuple-element.947, f32[512]{0:T(512)S(1)} %get-tuple-element.870), channel_id=1, replica_groups=mesh['dp'=2,'ctx'=32,'tp'=8] {'dp','ctx'}, use_global_device_ids=true, to_apply=%region_5.6 | all-reduce | flops 5120 | bytes 40960 | tf_op jit(solution)/shard_map/psum | solution.py:167
  382.3 4.2 fusion.94
  386.7 0.8 fusion.63
  387.5 6.4 copy.135
  393.9 1.7 while.56
  394.1 1.4 fusion.125
  395.7 2.0 while.57
  395.9 1.8 fusion.129
  398.0 3.4 while.58
  398.2 1.4 fusion.135
  399.6 1.8 fusion.136
  401.7 0.7 broadcast_in_dim_reshape.13
  402.4 140.3 %all_gather.21 = f32[4096,4]{1,0:T(8,128)S(1)} all-gather(f32[128,4]{1,0:T(8,128)S(1)} %copy.167), channel_id=1, replica_groups=mesh['dp'=2,'ctx'=32,'tp'=8] {'ctx'}, dimensions={0}, use_global_device_ids=true | all-gather | bytes 67584 | tf_op jit(solution)/shard_map/all_gather | solution.py:201
  543.4 74.2 %all_gather.20 = f32[4096,4]{0,1:T(4,128)S(1)} all-gather(f32[128,4]{0,1:T(4,128)S(1)} %bitcast.213), channel_id=1, replica_groups=mesh['dp'=2,'ctx'=32,'tp'=8] {'ctx'}, dimensions={0}, use_global_device_ids=true | all-gather | bytes 67584 | tf_op jit(solution)/shard_map/all_gather | solution.py:200
  617.7 25.9 %while.59 = (s32[]{:T(128)}, f32[128,4,128]{2,0,1:T(8,128)S(1)}, f32[128,4,128]{2,0,1:T(8,128)S(1)}, s32[]{:T(128)}, f32[4096,4]{0,1:T(4,128)S(1)}, /*index=5*/f...) while((s32[]{:T(128)}, f32[128,4,128]{2,0,1:T(8,128)S(1)}, ...), condition=%wide.region_22.23_spmd.clone.clone, body=%wide.region_19.22_spmd.clone.clone.sunk | while | flops 270729856 | bytes 7268725 | solution.py:248
  617.7 3.2 conditional.4
  617.8 1.3 constant_dynamic-slice_fusion
  619.7 0.8 fusion.17
  621.0 3.2 conditional.4
  621.0 1.3 constant_dynamic-slice_fusion
  623.0 0.8 fusion.17
  624.2 3.2 conditional.4
  624.2 1.3 constant_dynamic-slice_fusion
  626.2 0.8 fusion.17
  627.5 3.2 conditional.4
  627.5 1.3 constant_dynamic-slice_fusion
  629.4 0.8 fusion.17
  630.7 3.2 conditional.4
  630.7 1.3 constant_dynamic-slice_fusion
  632.7 0.8 fusion.17
  633.9 3.2 conditional.4
  633.9 1.3 constant_dynamic-slice_fusion
  635.9 0.8 fusion.17
  637.2 3.2 conditional.4
  637.2 1.3 constant_dynamic-slice_fusion
  639.1 0.8 fusion.17
  640.4 3.2 conditional.4
  640.4 1.3 constant_dynamic-slice_fusion
  642.4 0.8 fusion.17
  643.7 0.7 broadcast_in_dim_reshape.14
  645.3 0.8 copy.156
  (161 shorter events, 14.5 us)
Async XLA Ops:
  7.2 380.3 %all-gather.11.cloned.1.call-start = ((), (), s32[]{:S(2)}) async-start(), calls=%async_computation.1 | async-start | bytes 4325376 | tf_op jit(solution)/shard_map/all_gather | solution.py:103
  8.9 386.8 %all-gather.9.cloned.1.call-start = ((), (), s32[]{:S(2)}) async-start(), calls=%async_computation | async-start | bytes 4325376 | tf_op jit(solution)/shard_map/all_gather | solution.py:104
  10.7 607.0 %all-gather.13.cloned.1.call-start = ((), (), s32[]{:S(2)}) async-start(), calls=%async_computation.2 | async-start | bytes 4325376 | tf_op jit(solution)/shard_map/all_gather | solution.py:206
  12.4 605.2 %all-gather.15.cloned.1.call-start = ((), (), s32[]{:S(2)}) async-start(), calls=%async_computation.3 | async-start | bytes 4325376 | tf_op jit(solution)/shard_map/all_gather | solution.py:207
  13.5 36.3 %collective-permute-start = (bf16[127,512]{1,0:T(8,128)(2,1)S(1)}, bf16[127,512]{1,0:T(8,128)(2,1)S(1)}, u32[]{:S(2)}, u32[]{:S(2)}) collective-permute-start(bf16[127,512]{1,0:T(8,128)(2,1)S(1)} %slice_bitcast_fusion), channel_id=1, source_target_pairs={{0,8},{8,16},{16,24},{24,32},{32,40},{40,48},{48,56},{56,64},{64,7... | collective-permute-start | bytes 390152 | tf_op jit(solution)/shard_map/ppermute | solution.py:12
  24.5 9.7 %copy-start.1 = (bf16[1,128,512]{2,1,0:T(8,128)(2,1)S(1)}, bf16[1,128,512]{2,1,0:T(8,128)(2,1)}, u32[]{:S(2)}) copy-start(bf16[1,128,512]{2,1,0:T(8,128)(2,1)} %param.29) | copy-start | bytes 393220
  24.5 9.8 %copy-start.3 = (bf16[1,128,512]{2,1,0:T(8,128)(2,1)S(1)}, bf16[1,128,512]{2,1,0:T(8,128)(2,1)}, u32[]{:S(2)}) copy-start(bf16[1,128,512]{2,1,0:T(8,128)(2,1)} %param.25) | copy-start | bytes 393220
  24.5 9.9 %copy-start = (bf16[1,128,512]{2,1,0:T(8,128)(2,1)S(1)}, bf16[1,128,512]{2,1,0:T(8,128)(2,1)}, u32[]{:S(2)}) copy-start(bf16[1,128,512]{2,1,0:T(8,128)(2,1)} %param.23) | copy-start | bytes 393220
  24.6 10.0 %copy-start.10 = (f32[512]{0:T(512)S(1)}, f32[512]{0:T(512)}, u32[]{:S(2)}) copy-start(f32[512]{0:T(512)} %param.28) | copy-start | bytes 6148
  24.6 10.1 %copy-start.11 = (f32[512]{0:T(512)S(1)}, f32[512]{0:T(512)}, u32[]{:S(2)}) copy-start(f32[512]{0:T(512)} %param.27) | copy-start | bytes 6148
  24.6 10.2 %copy-start.9 = (f32[32,128]{1,0:T(8,128)S(1)}, f32[32,128]{1,0:T(8,128)}, u32[]{:S(2)}) copy-start(f32[32,128]{1,0:T(8,128)} %param.26) | copy-start | bytes 49156
  39.7 9.5 %copy-start.4 = (bf16[1,128,512]{1,2,0:T(8,128)(2,1)S(1)}, bf16[1,128,512]{1,2,0:T(8,128)(2,1)}, u32[]{:S(2)}) copy-start(bf16[1,128,512]{1,2,0:T(8,128)(2,1)} %copy.131) | copy-start | bytes 393220
  39.7 9.6 %copy-start.2 = (bf16[1,128,512]{1,2,0:T(8,128)(2,1)S(1)}, bf16[1,128,512]{1,2,0:T(8,128)(2,1)}, u32[]{:S(2)}) copy-start(bf16[1,128,512]{1,2,0:T(8,128)(2,1)} %copy.137) | copy-start | bytes 393220
  39.7 9.7 %copy-start.6 = (bf16[1,128,512]{1,2,0:T(8,128)(2,1)S(1)}, bf16[1,128,512]{1,2,0:T(8,128)(2,1)}, u32[]{:S(2)}) copy-start(bf16[1,128,512]{1,2,0:T(8,128)(2,1)} %copy.130) | copy-start | bytes 393220
  39.7 9.9 %copy-start.5 = (bf16[1,128,512]{1,2,0:T(8,128)(2,1)S(1)}, bf16[1,128,512]{1,2,0:T(8,128)(2,1)}, u32[]{:S(2)}) copy-start(bf16[1,128,512]{1,2,0:T(8,128)(2,1)} %copy.129) | copy-start | bytes 393220
  96.0 286.1 %collective-permute-start.1 = (bf16[127,512]{1,0:T(8,128)(2,1)S(1)}, bf16[127,512]{1,0:T(8,128)(2,1)S(1)}, u32[]{:S(2)}, u32[]{:S(2)}) collective-permute-start(bf16[127,512]{1,0:T(8,128)(2,1)S(1)} %bitcast.212), channel_id=1, source_target_pairs={{8,0},{16,8},{24,16},{32,24},{40,32},{48,40},{56,48},{64,56},{72,6... | collective-permute-start | bytes 390152 | tf_op jit(solution)/shard_map/ppermute | solution.py:12
  101.8 284.8 %copy-start.7 = (bf16[1,128,512]{2,1,0:T(8,128)(2,1)S(1)}, bf16[1,128,512]{2,1,0:T(8,128)(2,1)}, u32[]{:S(2)}) copy-start(bf16[1,128,512]{2,1,0:T(8,128)(2,1)} %param.24) | copy-start | bytes 393220
  101.8 284.8 %copy-start.8 = (bf16[1,128,512]{2,1,0:T(8,128)(2,1)S(1)}, bf16[1,128,512]{2,1,0:T(8,128)(2,1)}, u32[]{:S(2)}) copy-start(bf16[1,128,512]{2,1,0:T(8,128)(2,1)} %param.22) | copy-start | bytes 393220
Sparse Core Ops, SparseCore 0:
  10.6 144.1 all-gather.10
  157.4 139.1 all-gather.8
  299.2 141.8 all-gather.12
  443.5 144.5 all-gather.14
where the time goes:
time: 654 us; the launch traced here: 653 us
  blocking collectives  520 us (80%)
  local copies, waits for them, and re-layouts  70.3 us (11%)
  matrix products  31.3 us (5%)
  between operations  14.2 us (2%)
  starting transfers between devices  8.48 us (1%)
  other arithmetic  6.97 us (1%)
    psum x1, blocking collectives, shards(): lax.psum((filter_part, skip_part, gain_part), ('dp', 'ctx'))  278 us
    all_gather x1, blocking collectives, shards(): lax.all_gather(delta.T, 'ctx', axis=0, tiled=True)  140 us
    all_gather x1, blocking collectives, shards(): lax.all_gather(log_norm.T, 'ctx', axis=0, tiled=True)  74.2 us
    unnamed x40, local copies, waits for them, and re-layouts  23.3 us
    reshape x2, local copies, waits for them, and re-layouts, toeplitz(): return tiled.reshape(groups, rows, width)  19.1 us
    psum x1, blocking collectives, shards(): square_total = lax.psum(jnp.sum(stream * stream, axis=1), 'tp')  14.4 us
  transfers between devices with their start and end apart: 6, of which 0 were waited for; matrix products, arithmetic and copies ran while one was open for 12% of the time, Pallas kernels for 0%

commit v1 on v0

--- a/solution.py
+++ b/solution.py
@@ -4,6 +4,13 @@
 from jax.sharding import PartitionSpec as P
 
 HEAD_DIM = 128
+
+
+def exchange_gather(x, axis, d):
+    peers = lax.axis_size(axis)
+    blocks = jnp.stack([x for _ in range(peers)])
+    blocks = lax.all_to_all(blocks, axis, split_axis=0, concat_axis=0)
+    return jnp.concatenate(blocks, axis=d)
 
 
 def passed_along(value, axis, steps):
@@ -197,7 +204,7 @@
     )
     grad_queries = (query_grad * scale).astype(jnp.bfloat16)
     stat_norm, stat_delta = (
-        lax.all_gather(log_norm.T, "ctx", axis=0, tiled=True),
+        exchange_gather(log_norm.T, "ctx", 0),
         lax.all_gather(delta.T, "ctx", axis=0, tiled=True),
     )
     key_own = attn_keys[0].reshape(rows, heads_here, HEAD_DIM)

time: 654 us -> 627 us (0.959)
  the two profiles are of different devices: /device:TPU:8 before, /device:TPU:6 now
where the time goes in v1:
time: 627 us; the launch traced here: 625 us
  blocking collectives  405 us (65%)
  local copies, waits for them, and re-layouts  70.9 us (11%)
  starting transfers between devices  54.2 us (9%)
  waiting for transfers between devices  40.8 us (7%)
  matrix products  31.4 us (5%)
  between operations  14.2 us (2%)
  other arithmetic  6.98 us (1%)
    psum x1, blocking collectives, shards(): lax.psum((filter_part, skip_part, gain_part), ('dp', 'ctx'))  285 us
    all_gather x1, blocking collectives, shards(): lax.all_gather(delta.T, 'ctx', axis=0, tiled=True)  94.8 us
    all_to_all x1, starting transfers between devices, exchange_gather(): blocks = lax.all_to_all(blocks, axis, split_axis=0, concat_axis=0)  49.3 us
    all_gather x1, waiting for transfers between devices, shards(): piece_grad = lax.all_gather(attended_grad[0], 'ctx', axis=0, tiled=True)  40.7 us
    unnamed x40, local copies, waits for them, and re-layouts  23.3 us
    reshape x2, local copies, waits for them, and re-layouts, toeplitz(): return tiled.reshape(groups, rows, width)  19.1 us
    psum x1, blocking collectives, shards(): norm_dot = lax.psum(jnp.sum(gain_grad * scaled, axis=1), 'tp')  13.2 us
  transfers between devices with their start and end apart: 7, of which 1 were waited for; matrix products, arithmetic and copies ran while one was open for 13% of the time, Pallas kernels for 0%

profile of v1, /device:TPU:6, one launch (start us, length us, event | category | flops | bytes accessed | tf_op | source)
XLA Modules:
  0.0 624.9 jit_solution(15356956441379156511)
XLA Ops:
  7.2 1.7 copy.130
  9.0 1.7 copy.129
  10.7 1.7 copy.131
  12.4 1.0 fusion.64
  13.5 3.5 collective-permute-start
  17.0 1.7 copy.137
  18.8 0.8 rev.6
  19.9 2.4 copy.177
  22.4 2.2 slice.25
  24.6 9.6 %reshape.390 = f32[32,128,255]{2,1,0:T(8,128)} reshape(f32[32,32640]{1,0:T(8,128)} %slice.25) | data formatting | bytes 8355840 | tf_op jit(solution)/shard_map/reshape | solution.py:27
  35.1 2.4 copy.178
  37.5 2.2 slice.27
  39.8 9.5 %reshape.394 = f32[32,128,255]{2,1,0:T(8,128)} reshape(f32[32,32640]{1,0:T(8,128)} %slice.27) | data formatting | bytes 8355840 | tf_op jit(solution)/shard_map/reshape | solution.py:27
  50.0 4.3 fusion.93
  54.6 12.1 %psum.35 = f32[128]{0:T(128)S(1)} all-reduce(f32[128]{0:T(128)S(1)} %get-tuple-element.951), channel_id=1, replica_groups=mesh['dp'=2,'ctx'=32,'tp'=8] {'tp'}, use_global_device_ids=true, to_apply=%region_1.2 | all-reduce | flops 128 | bytes 1024 | tf_op jit(solution)/shard_map/psum | solution.py:136
  66.9 13.2 %psum.36 = f32[128]{0:T(128)S(1)} all-reduce(f32[128]{0:T(128)S(1)} %get-tuple-element.871), channel_id=1, replica_groups=mesh['dp'=2,'ctx'=32,'tp'=8] {'tp'}, use_global_device_ids=true, to_apply=%region_3.4 | all-reduce | flops 128 | bytes 1024 | tf_op jit(solution)/shard_map/psum | solution.py:142
  80.3 3.1 fusion.81
  83.4 5.2 reshape.396
  88.6 2.5 pad.13
  91.1 3.2 copy.179
  94.3 1.3 collective-permute-start.1
  95.8 0.8 fusion.90
  96.6 1.8 slice_reduce_fusion
  98.5 285.1 %all-reduce.3 = (f32[32,128]{1,0:T(8,128)}, f32[512]{0:T(512)}, f32[512]{0:T(512)}) all-reduce(f32[32,128]{1,0:T(8,128)S(1)} %rev.7, f32[512]{0:T(512)S(1)} %get-tuple-element.947, f32[512]{0:T(512)S(1)} %get-tuple-element.870), channel_id=1, replica_groups=mesh['dp'=2,'ctx'=32,'tp'=8] {'dp','ctx'}, use_global_device_ids=true, to_apply=%region_5.6 | all-reduce | flops 5120 | bytes 40960 | tf_op jit(solution)/shard_map/psum | solution.py:174
  383.7 4.2 fusion.94
  388.1 0.8 fusion.63
  389.0 6.4 %copy.135 = bf16[4096,4,128]{2,0,1:T(8,128)(2,1)} copy(bf16[4096,4,128]{0,2,1:T(8,128)(2,1)} %bitcast.194) | data formatting | bytes 8388608
  395.3 1.7 while.56
  395.5 1.4 fusion.125
  397.1 2.0 while.57
  397.3 1.8 fusion.129
  399.5 3.4 while.58
  399.6 1.4 fusion.135
  401.1 1.8 fusion.136
  403.6 49.3 %all-to-all-start = ((f32[32,128,4]{1,2,0:T(4,128)}), f32[32,128,4]{1,2,0:T(4,128)S(1)}, u32[]{:S(2)}, u32[]{:S(2)}) async-start(f32[32,128,4]{1,2,0:T(4,128)} %stack.2), calls=%async_computation | async-start | bytes 131072 | tf_op jit(solution)/shard_map/all_to_all | solution.py:12
  453.1 0.7 broadcast_in_dim_reshape.13
  453.8 94.8 %all_gather.17 = f32[4096,4]{1,0:T(8,128)S(1)} all-gather(f32[128,4]{1,0:T(8,128)S(1)} %copy.167), channel_id=1, replica_groups=mesh['dp'=2,'ctx'=32,'tp'=8] {'ctx'}, dimensions={0}, use_global_device_ids=true | all-gather | bytes 67584 | tf_op jit(solution)/shard_map/all_gather | solution.py:208
  549.2 0.8 copy.156
  550.0 40.7 %all-gather.15.cloned.1.call-done = bf16[1,4096,512]{1,2,0:T(8,128)(2,1)} async-done(((bf16[1,128,512]{1,2,0:T(8,128)(2,1)}), bf16[1,4096,512]{1,2,0:T(8,128)(2,1)}) %all-gather.15.cloned.1.call-update) | async-done | bytes 4194320 | tf_op jit(solution)/shard_map/all_gather | solution.py:214
  590.7 25.9 %while.59 = (s32[]{:T(128)}, f32[128,4,128]{2,0,1:T(8,128)S(1)}, f32[128,4,128]{2,0,1:T(8,128)S(1)}, s32[]{:T(128)}, f32[4096,4]{0,1:T(4,128)S(1)}, /*index=5*/f...) while((s32[]{:T(128)}, f32[128,4,128]{2,0,1:T(8,128)S(1)}, ...), condition=%wide.region_22.23_spmd.clone.clone, body=%wide.region_19.22_spmd.clone.clone.sunk | while | flops 270729856 | bytes 7268725 | solution.py:255
  590.8 3.2 conditional.4
  590.8 1.3 constant_dynamic-slice_fusion
  592.8 0.8 fusion.17
  594.0 3.2 conditional.4
  594.0 1.3 constant_dynamic-slice_fusion
  596.0 0.8 fusion.17
  597.3 3.2 conditional.4
  597.3 1.3 constant_dynamic-slice_fusion
  599.3 0.8 fusion.17
  600.5 3.2 conditional.4
  600.5 1.3 constant_dynamic-slice_fusion
  602.5 0.8 fusion.17
  603.8 3.2 conditional.4
  603.8 1.3 constant_dynamic-slice_fusion
  605.7 0.8 fusion.17
  607.0 3.2 conditional.4
  607.0 1.3 constant_dynamic-slice_fusion
  609.0 0.8 fusion.17
  610.2 3.2 conditional.4
  610.3 1.3 constant_dynamic-slice_fusion
  612.2 0.8 fusion.17
  613.5 3.2 conditional.4
  613.5 1.3 constant_dynamic-slice_fusion
  615.5 0.8 fusion.17
  (163 shorter events, 15.9 us)
Async XLA Ops:
  7.2 381.8 %all-gather.11.cloned.1.call-start = ((), (), s32[]{:S(2)}) async-start(), calls=%async_computation.2 | async-start | bytes 4325376 | tf_op jit(solution)/shard_map/all_gather | solution.py:110
  8.9 388.2 %all-gather.9.cloned.1.call-start = ((), (), s32[]{:S(2)}) async-start(), calls=%async_computation.1 | async-start | bytes 4325376 | tf_op jit(solution)/shard_map/all_gather | solution.py:111
  10.7 539.3 %all-gather.13.cloned.1.call-start = ((), (), s32[]{:S(2)}) async-start(), calls=%async_computation.3 | async-start | bytes 4325376 | tf_op jit(solution)/shard_map/all_gather | solution.py:213
  12.4 578.3 %all-gather.15.cloned.1.call-start = ((), (), s32[]{:S(2)}) async-start(), calls=%async_computation.4 | async-start | bytes 4325376 | tf_op jit(solution)/shard_map/all_gather | solution.py:214
  13.5 36.3 %collective-permute-start = (bf16[127,512]{1,0:T(8,128)(2,1)S(1)}, bf16[127,512]{1,0:T(8,128)(2,1)S(1)}, u32[]{:S(2)}, u32[]{:S(2)}) collective-permute-start(bf16[127,512]{1,0:T(8,128)(2,1)S(1)} %slice_bitcast_fusion), channel_id=1, source_target_pairs={{0,8},{8,16},{16,24},{24,32},{32,40},{40,48},{48,56},{56,64},{64,7... | collective-permute-start | bytes 390152 | tf_op jit(solution)/shard_map/ppermute | solution.py:19
  24.6 9.7 %copy-start.1 = (bf16[1,128,512]{2,1,0:T(8,128)(2,1)S(1)}, bf16[1,128,512]{2,1,0:T(8,128)(2,1)}, u32[]{:S(2)}) copy-start(bf16[1,128,512]{2,1,0:T(8,128)(2,1)} %param.29) | copy-start | bytes 393220
  24.6 9.8 %copy-start.3 = (bf16[1,128,512]{2,1,0:T(8,128)(2,1)S(1)}, bf16[1,128,512]{2,1,0:T(8,128)(2,1)}, u32[]{:S(2)}) copy-start(bf16[1,128,512]{2,1,0:T(8,128)(2,1)} %param.25) | copy-start | bytes 393220
  24.6 9.9 %copy-start = (bf16[1,128,512]{2,1,0:T(8,128)(2,1)S(1)}, bf16[1,128,512]{2,1,0:T(8,128)(2,1)}, u32[]{:S(2)}) copy-start(bf16[1,128,512]{2,1,0:T(8,128)(2,1)} %param.23) | copy-start | bytes 393220
  24.6 10.0 %copy-start.10 = (f32[512]{0:T(512)S(1)}, f32[512]{0:T(512)}, u32[]{:S(2)}) copy-start(f32[512]{0:T(512)} %param.28) | copy-start | bytes 6148
  24.6 10.1 %copy-start.11 = (f32[512]{0:T(512)S(1)}, f32[512]{0:T(512)}, u32[]{:S(2)}) copy-start(f32[512]{0:T(512)} %param.27) | copy-start | bytes 6148
  24.6 10.1 %copy-start.9 = (f32[32,128]{1,0:T(8,128)S(1)}, f32[32,128]{1,0:T(8,128)}, u32[]{:S(2)}) copy-start(f32[32,128]{1,0:T(8,128)} %param.26) | copy-start | bytes 49156
  39.7 9.5 %copy-start.4 = (bf16[1,128,512]{1,2,0:T(8,128)(2,1)S(1)}, bf16[1,128,512]{1,2,0:T(8,128)(2,1)}, u32[]{:S(2)}) copy-start(bf16[1,128,512]{1,2,0:T(8,128)(2,1)} %copy.131) | copy-start | bytes 393220
  39.7 9.6 %copy-start.2 = (bf16[1,128,512]{1,2,0:T(8,128)(2,1)S(1)}, bf16[1,128,512]{1,2,0:T(8,128)(2,1)}, u32[]{:S(2)}) copy-start(bf16[1,128,512]{1,2,0:T(8,128)(2,1)} %copy.137) | copy-start | bytes 393220
  39.7 9.8 %copy-start.6 = (bf16[1,128,512]{1,2,0:T(8,128)(2,1)S(1)}, bf16[1,128,512]{1,2,0:T(8,128)(2,1)}, u32[]{:S(2)}) copy-start(bf16[1,128,512]{1,2,0:T(8,128)(2,1)} %copy.130) | copy-start | bytes 393220
  39.8 9.9 %copy-start.5 = (bf16[1,128,512]{1,2,0:T(8,128)(2,1)S(1)}, bf16[1,128,512]{1,2,0:T(8,128)(2,1)}, u32[]{:S(2)}) copy-start(bf16[1,128,512]{1,2,0:T(8,128)(2,1)} %copy.129) | copy-start | bytes 393220
  94.3 289.2 %collective-permute-start.1 = (bf16[127,512]{1,0:T(8,128)(2,1)S(1)}, bf16[127,512]{1,0:T(8,128)(2,1)S(1)}, u32[]{:S(2)}, u32[]{:S(2)}) collective-permute-start(bf16[127,512]{1,0:T(8,128)(2,1)S(1)} %bitcast.213), channel_id=1, source_target_pairs={{8,0},{16,8},{24,16},{32,24},{40,32},{48,40},{56,48},{64,56},{72,6... | collective-permute-start | bytes 390152 | tf_op jit(solution)/shard_map/ppermute | solution.py:19
  96.6 291.5 %copy-start.7 = (bf16[1,128,512]{2,1,0:T(8,128)(2,1)S(1)}, bf16[1,128,512]{2,1,0:T(8,128)(2,1)}, u32[]{:S(2)}) copy-start(bf16[1,128,512]{2,1,0:T(8,128)(2,1)} %param.24) | copy-start | bytes 393220
  96.6 291.5 %copy-start.8 = (bf16[1,128,512]{2,1,0:T(8,128)(2,1)S(1)}, bf16[1,128,512]{2,1,0:T(8,128)(2,1)}, u32[]{:S(2)}) copy-start(bf16[1,128,512]{2,1,0:T(8,128)(2,1)} %param.22) | copy-start | bytes 393220
  403.6 187.0 %all-to-all-start = ((f32[32,128,4]{1,2,0:T(4,128)}), f32[32,128,4]{1,2,0:T(4,128)S(1)}, u32[]{:S(2)}, u32[]{:S(2)}) async-start(f32[32,128,4]{1,2,0:T(4,128)} %stack.2), calls=%async_computation | async-start | bytes 131072 | tf_op jit(solution)/shard_map/all_to_all | solution.py:12
Sparse Core Ops, SparseCore 0:
  10.6 146.1 all-gather.10
  159.4 137.5 all-gather.8
  299.0 139.1 all-gather.12
  440.6 150.0 all-gather.14
